TPU v7x, 512 devices: a whole 4x8x8 slice. The times are simulated.
512 devices in a mesh: row: 16 (over y_lo, x, core), col: 8 (over z), seq: 4 (over y_hi).
Axes of the slice: x: 4, y: 8 (y_hi: 4, y_lo: 2; y = y_hi * 2 + y_lo), z: 8, core: 2. Of those that a mesh axis runs over, the one named last changes fastest.
Arguments:
- left_piece: bfloat16 [512, 32, 1024], P('seq', None, 'row'), may hold values from -6 to 6
- right_piece: bfloat16 [512, 32, 1024], P('seq', 'row', 'col'), may hold values from -6 to 6
- proj_weight: bfloat16 [1024, 128], replicated, may hold values from -4 to 4
- proj_bias: float32 [128], replicated, may hold values from -3 to 3
- pair_rep: bfloat16 [1024, 1024, 128], P(('row', 'seq'), 'col'), may hold values from -6 to 6
- norm_gain: float32 [128], replicated, may hold values from 0.5 to 1.5
- up_weight: bfloat16 [128, 512], replicated, may hold values from -0.5 to 0.5
- up_bias: float32 [512], replicated, may hold values from -3 to 3
- down_weight: bfloat16 [512, 128], replicated, may hold values from -0.25 to 0.25
- down_bias: float32 [128], replicated, may hold values from -3 to 3
Outputs:
- refined: bfloat16 [1024, 1024, 128], P(('row', 'seq'), 'col')
All inputs are finite; a program needn't handle non-finite values.
Results may differ from a plain program's by a relative error of at most 0.0085.
Values may be sent and summed in bfloat16 or wider, within the bound.
A program may use at most 64 MiB of HBM per device.

v0:
```python
import jax
import jax.numpy as jnp
from jax import lax
from jax.sharding import PartitionSpec as P

epsilon = 1e-05


def project_block(row_slab, right_all, proj_weight):
    seq_count, channels, row_count = row_slab.shape
    columns = right_all.shape[2]
    left_mat = row_slab.reshape(seq_count, channels * row_count)
    right_mat = right_all.reshape(seq_count, channels * columns)
    outer_prod = lax.dot_general(
        left_mat, right_mat, (((0,), (0,)), ((), ())), preferred_element_type=jnp.float32
    ).astype(jnp.bfloat16)
    outer_prod = outer_prod.reshape(channels, row_count, channels, columns).transpose(1, 3, 0, 2)
    outer_prod = outer_prod.reshape(row_count * columns, channels * channels)
    result = jnp.dot(outer_prod, proj_weight, preferred_element_type=jnp.float32)
    return result.reshape(row_count, columns, proj_weight.shape[1])


def project_rows(row_slab, right_all, proj_weight):
    seq_count, channels, row_count = row_slab.shape
    sub_rows = 8
    pieces = row_slab.reshape(seq_count, channels, row_count // sub_rows, sub_rows)
    pieces = jnp.moveaxis(pieces, 2, 0)
    result = lax.map(lambda portion: project_block(portion, right_all, proj_weight), pieces)
    return result.reshape(row_count, right_all.shape[2], proj_weight.shape[1])


def transition(middle, norm_gain, up_weight, up_bias, down_weight, down_bias):
    row_count, columns, channels = middle.shape
    values = middle.astype(jnp.float32).reshape(row_count * columns, channels)
    center = jnp.mean(values, axis=1, keepdims=True)
    spread = jnp.mean(jnp.square(values - center), axis=1, keepdims=True)
    normed = ((values - center) * lax.rsqrt(spread + epsilon) * norm_gain).astype(jnp.bfloat16)
    hidden = jnp.maximum(
        jnp.dot(normed, up_weight, preferred_element_type=jnp.float32) + up_bias, 0.0
    ).astype(jnp.bfloat16)
    result = values + jnp.dot(hidden, down_weight, preferred_element_type=jnp.float32) + down_bias
    return result.astype(jnp.bfloat16).reshape(row_count, columns, channels)


def gather_right(right_part):
    return lax.all_gather(right_part, "row", axis=1, tiled=True)


def move_cols(tile):
    return lax.all_to_all(tile, "col", split_axis=0, concat_axis=2, tiled=True)


def on_device(
    left_piece,
    right_piece,
    proj_weight,
    proj_bias,
    pair_rep,
    norm_gain,
    up_weight,
    up_bias,
    down_weight,
    down_bias,
):
    own_rows = pair_rep.shape[0]
    columns = pair_rep.shape[1]
    channels = pair_rep.shape[2]
    groups = lax.axis_size("seq")
    seq_index = lax.axis_index("seq")
    group_len = left_piece.shape[0]
    seq_total = group_len * groups
    left_all, right_seq = (
        lax.all_gather(left_piece, "seq", axis=0, tiled=True),
        lax.all_gather(right_piece, "seq", axis=0, tiled=True),
    )
    right_all = gather_right(right_seq)
    offset = seq_index * own_rows
    summed = jnp.zeros((own_rows, columns, channels), jnp.float32)
    for group_id in range(groups):
        left_group = left_all[group_id * group_len : (group_id + 1) * group_len]
        row_slab = lax.dynamic_slice_in_dim(left_group, offset, own_rows, 2)
        right_group = right_all[group_id * group_len : (group_id + 1) * group_len]
        summed = summed + project_rows(row_slab, right_group, proj_weight)
    update = (summed / seq_total + proj_bias).astype(jnp.bfloat16)
    col_count = lax.axis_size("col")
    rowseq_count = lax.axis_size(("row", "seq"))
    run_len = own_rows // col_count
    section_one = move_cols(update.reshape(col_count, run_len, columns, channels))
    section_two = lax.all_to_all(
        section_one.reshape(run_len, rowseq_count, own_rows, channels),
        ("row", "seq"),
        split_axis=1,
        concat_axis=0,
        tiled=True,
    )
    section_three = move_cols(
        section_two.reshape(col_count, rowseq_count // col_count, 1, run_len, own_rows, channels)
    )
    mirrored = section_three.reshape(columns, own_rows, channels).transpose(1, 0, 2)
    middle = (
        pair_rep.astype(jnp.float32)
        + 0.5 * (update.astype(jnp.float32) + mirrored.astype(jnp.float32))
    ).astype(jnp.bfloat16)
    return transition(middle, norm_gain, up_weight, up_bias, down_weight, down_bias)


def solution(mesh):
    in_specs = (
        P("seq", None, "row"),
        P("seq", "row", "col"),
        P(),
        P(),
        P(("row", "seq"), "col", None),
        P(),
        P(),
        P(),
        P(),
        P(),
    )
    out_specs = P(("row", "seq"), "col", None)
    return jax.shard_map(
        on_device, mesh=mesh, in_specs=in_specs, out_specs=out_specs, check_vma=False
    )
```

profile of v0, /device:TPU:1, one launch (start us, length us, event | category | flops | bytes accessed | tf_op | source)
XLA Modules:
  0.0 234.8 jit_solution(6227691487281684803)
XLA Ops:
  6.5 0.7 all-gather.3.cloned.1.call-update
  7.3 0.0 all-gather.5.cloned.1.call-start
  7.3 15.7 %all_gather.10 = bf16[512,2,128]{2,1,0:T(2,128)(2,1)S(1)} all-gather(bf16[128,2,128]{2,1,0:T(2,128)(2,1)} %param.19), channel_id=1, replica_groups=mesh['row'=16,'col'=8,'seq'=4] {'seq'}, dimensions={0}, use_global_device_ids=true | all-gather | bytes 327680 | tf_op jit(solution)/shard_map/all_gather | solution.py:74
  23.0 0.7 copy.100
  23.7 0.0 all-gather.5.cloned.1.call-update
  23.8 43.0 %all-gather.3.cloned.1.call-done = bf16[512,32,64]{0,2,1:T(8,128)(2,1)} async-done(((bf16[128,32,64]{0,2,1:T(8,128)(2,1)}), bf16[512,32,64]{0,2,1:T(8,128)(2,1)}) %all-gather.3.cloned.1.call-update) | async-done | bytes 2097168 | tf_op jit(solution)/shard_map/all_gather | solution.py:73
  66.7 1.8 fusion.68
  68.5 0.7 dynamic-slice_bitcast_fusion.2
  69.2 0.7 dynamic-slice_bitcast_fusion
  69.9 46.1 %all-gather.5.cloned.1.call-done = bf16[512,32,128]{2,0,1:T(8,128)(2,1)} async-done(((bf16[512,2,128]{2,0,1:T(8,128)(2,1)}), bf16[512,32,128]{2,0,1:T(8,128)(2,1)}) %all-gather.5.cloned.1.call-update) | async-done | bytes 4194320 | tf_op jit(solution)/shard_map/all_gather | solution.py:46
  116.0 2.8 %fusion.67 = (bf16[128,32,128]{2,0,1:T(8,128)(2,1)S(1)}, bf16[128,32,128]{2,0,1:T(8,128)(2,1)S(1)}, bf16[128,32,128]{2,0,1:T(8,128)(2,1)S(1)}, bf16[128,32,128]{2,0,1:T(8,128)(2,1)S(1)}) fusion(bf16[512,32,128]{2,0,1:T(8,128)(2,1)} %all-gather.5.cloned.1.call-done), kind=kLoop, calls=%fused_computation.71 | loop fusion | bytes 8388608 | tf_op jit(solution)/shard_map/slice | solution.py:82
  118.8 0.7 copy.104
  119.5 0.7 copy.108
  120.2 0.7 copy.106
  120.9 1.7 copy.102
  122.6 1.1 broadcast.42.clone.2
  123.7 7.8 %while.40 = (s32[]{:T(128)}, f32[2,8,128,128]{3,2,1,0:T(8,128)}, bf16[2,128,32,8]{1,3,0,2:T(8,128)(2,1)}, bf16[128,32,128]{2,1,0:T(8,128)(2,1)}, bf16[1024,128]{1,0:T(8,128)(2,1)}, /*index=5*/s32[]{:T(128)}) while((s32[]{:T(128)}, f32[2,8,128,128]{3,2,1,0:T(8,128)}, bf16[2,128,32,8]{1,3,0,2:T(8,128)(2,1)}, bf16[128,32,128]{2,1,0:T(8,128)(2,1)}, ...), condition=%wide.region_1.2_spmd, body=%wide.region_0.1_spmd.sunk | while | flops 537919488 | bytes 15532201 | solution.py:28
  123.7 2.1 convolution_convert_fusion.8
  125.8 0.8 fusion.96
  126.6 1.0 copy-done.2
  127.6 2.1 convolution_convert_fusion.8
  129.7 0.8 fusion.96
  130.5 1.0 copy-done.2
  131.5 1.1 broadcast.42.clone.1
  132.5 6.9 %while.42 = (s32[]{:T(128)}, f32[2,8,128,128]{3,2,1,0:T(8,128)}, bf16[2,128,32,8]{1,3,0,2:T(8,128)(2,1)}, bf16[128,32,128]{2,1,0:T(8,128)(2,1)S(1)}, bf16[1024,128]{1,0:T(8,128)(2,1)}, /*index=5*/s32[]{:T(128)}) while((s32[]{:T(128)}, f32[2,8,128,128]{3,2,1,0:T(8,128)}, bf16[2,128,32,8]{1,3,0,2:T(8,128)(2,1)}, ...), condition=%wide.region_5.6_spmd, body=%wide.region_4.5_spmd.sunk | while | flops 537919488 | bytes 15532201 | solution.py:28
  132.5 1.7 convolution_convert_fusion.10
  134.2 0.8 fusion.106
  135.0 1.0 copy-done.5
  136.0 1.7 convolution_convert_fusion.10
  137.7 0.8 fusion.106
  138.5 1.0 copy-done.5
  139.5 0.1 broadcast.42.clone
  139.6 3.5 %while.43 = (s32[]{:T(128)}, f32[2,8,128,128]{3,2,1,0:T(8,128)S(1)}, bf16[2,128,32,8]{1,3,0,2:T(8,128)(2,1)S(1)}, bf16[128,32,128]{2,1,0:T(8,128)(2,1)S(1)}, bf16[1024,128]{1,0:T(8,128)(2,1)}, /*index=5*/s32[]{:T(128)}) while((s32[]{:T(128)}, f32[2,8,128,128]{3,2,1,0:T(8,128)S(1)}, bf16[2,128,32,8]{1,3,0,2:T(8,128)(2,1)S(1)}, ...), condition=%wide.region_7.8_spmd, body=%wide.region_6.7_spmd.sunk | while | flops 537919488 | bytes 7143537 | solution.py:28
  139.6 0.7 convolution_convert_fusion.11
  140.3 0.2 copy-done.12
  140.5 0.8 fusion.111
  141.3 0.8 convolution_convert_fusion.11
  142.1 0.2 copy-done.12
  142.3 0.8 fusion.111
  143.1 0.1 broadcast.42.clone.3
  143.2 0.9 copy-done.6
  144.1 3.6 %while.41 = (s32[]{:T(128)}, f32[2,8,128,128]{3,2,1,0:T(8,128)S(1)}, bf16[2,128,32,8]{1,3,0,2:T(8,128)(2,1)S(1)}, bf16[128,32,128]{2,1,0:T(8,128)(2,1)S(1)}, bf16[1024,128]{1,0:T(8,128)(2,1)}, /*index=5*/s32[]{:T(128)}) while((s32[]{:T(128)}, f32[2,8,128,128]{3,2,1,0:T(8,128)S(1)}, bf16[2,128,32,8]{1,3,0,2:T(8,128)(2,1)S(1)}, ...), condition=%wide.region_3.4_spmd, body=%wide.region_2.3_spmd.sunk | while | flops 537919488 | bytes 7143537 | solution.py:28
  144.1 0.7 convolution_convert_fusion.9
  144.8 0.3 copy-done.13
  145.1 0.8 fusion.101
  145.9 0.8 convolution_convert_fusion.9
  146.7 0.2 copy-done.13
  146.9 0.8 fusion.101
  147.7 1.8 add_multiply_fusion
  149.6 0.1 add_convert_fusion
  149.7 24.2 %all_to_all.39 = bf16[8,2,128,128]{3,2,1,0:T(8,128)(2,1)S(1)} all-to-all(bf16[8,2,128,128]{3,2,1,0:T(8,128)(2,1)S(1)} %add_convert_fusion), channel_id=1, replica_groups=mesh['row'=16,'col'=8,'seq'=4] {'col'}, dimensions={0} | all-to-all | bytes 1048576 | tf_op jit(solution)/shard_map/all_to_all | solution.py:50
  174.0 28.1 %all_to_all.40 = bf16[2,64,16,128]{3,2,0,1:T(8,128)(2,1)S(1)} all-to-all(bf16[2,64,16,128]{3,2,0,1:T(8,128)(2,1)S(1)} %copy.111), channel_id=1, replica_groups=mesh['row'=16,'col'=8,'seq'=4] {'row','seq'}, dimensions={1} | all-to-all | bytes 1048576 | tf_op jit(solution)/shard_map/all_to_all | solution.py:89
  202.1 20.6 %all_to_all.41 = bf16[8,8,1,2,16,128]{5,4,3,1,2,0:T(8,128)(2,1)S(1)} all-to-all(bf16[8,8,1,2,16,128]{5,4,3,1,2,0:T(8,128)(2,1)S(1)} %bitcast.205), channel_id=1, replica_groups=mesh['row'=16,'col'=8,'seq'=4] {'col'}, dimensions={0} | all-to-all | bytes 1048576 | tf_op jit(solution)/shard_map/all_to_all | solution.py:50
  222.7 0.1 bitcast_convert_fusion
  222.8 1.0 fusion.60
  223.8 0.3 convert_reduce_fusion
  224.2 0.1 copy.114
  224.3 0.1 copy.115
  224.4 0.1 copy.116
  224.5 0.6 multiply_reduce_fusion
  225.2 0.1 copy.117
  225.2 0.0 copy-done.9
  225.2 0.6 fusion.63
  225.9 2.0 fusion.57
  (45 shorter events, 0.2 us)
Async XLA Ops:
  6.5 219.3 %copy-start = (bf16[512,128]{1,0:T(8,128)(2,1)S(1)}, bf16[512,128]{1,0:T(8,128)(2,1)}, u32[]{:S(2)}) copy-start(bf16[512,128]{1,0:T(8,128)(2,1)} %param.26) | copy-start | bytes 393220
  6.5 60.2 %all-gather.3.cloned.1.call-start = ((), (), s32[]{:S(2)}) async-start(), calls=%async_computation.3 | async-start | bytes 2621440 | tf_op jit(solution)/shard_map/all_gather | solution.py:73
  7.3 108.8 %all-gather.5.cloned.1.call-start = ((), (), s32[]{:S(2)}) async-start(), calls=%async_computation.4 | async-start | bytes 4456448 | tf_op jit(solution)/shard_map/all_gather | solution.py:46
  123.7 2.1 copy-start.1
  123.7 2.1 copy-start.10
  126.6 1.0 copy-start.2
  127.6 2.1 copy-start.1
  127.6 2.1 copy-start.10
  130.5 1.0 copy-start.2
  132.5 1.7 copy-start.4
  132.5 1.7 copy-start.11
  135.0 1.0 copy-start.5
  136.0 1.7 copy-start.4
  136.0 1.7 copy-start.11
  138.5 1.0 copy-start.5
  139.6 1.0 copy-start.12
  141.3 1.0 copy-start.12
  143.1 1.0 copy-start.6
  144.1 3.6 %copy-start.3 = (f32[2,8,128,128]{3,2,1,0:T(8,128)S(1)}, f32[2,8,128,128]{3,2,1,0:T(8,128)}, u32[]{:S(2)}) copy-start(f32[2,8,128,128]{3,2,1,0:T(8,128)} %get-tuple-element.113) | copy-start | bytes 3145732
  144.1 1.0 copy-start.13
  145.9 1.0 copy-start.13
  147.7 1.9 copy-start.8
  174.0 48.8 %copy-start.7 = (bf16[16,128,128]{2,1,0:T(8,128)(2,1)S(1)}, bf16[16,128,128]{2,1,0:T(8,128)(2,1)}, u32[]{:S(2)}) copy-start(bf16[16,128,128]{2,1,0:T(8,128)(2,1)} %param.22) | copy-start | bytes 1572868
  223.8 1.4 copy-start.9
  224.2 1.7 copy-start.14
  224.2 1.7 copy-start.15
  224.2 1.7 copy-start.16
Sparse Core Ops, SparseCore 0:
  9.4 57.2 all-gather.2
  68.9 47.1 all-gather.4
where the time goes:
time: 235 us
  waiting for transfers between devices  89.8 us (38%)
  blocking collectives  88.6 us (38%)
  local copies, waits for them, and re-layouts  18.9 us (8%)
  matrix products  18.8 us (8%)
  between operations  13.7 us (6%)
  other arithmetic  4.69 us (2%)
    all_gather x1, waiting for transfers between devices, gather_right(): return lax.all_gather(right_part, 'row', axis=1, tiled=True)  46.1 us
    all_to_all x2, blocking collectives, move_cols(): return lax.all_to_all(tile, 'col', split_axis=0, concat_axis=2, tiled=True)  44.8 us
    all_gather x1, waiting for transfers between devices, on_device(): lax.all_gather(left_piece, 'seq', axis=0, tiled=True)  43 us
    all_to_all x1, blocking collectives, on_device(): lax.all_to_all(section_one.reshape(run_len, rowseq_count, own_rows, chann...  28.1 us
    all_gather x1, blocking collectives, on_device(): lax.all_gather(right_piece, 'seq', axis=0, tiled=True)  15.7 us
    dot_general x8, matrix products, project_block(): lax.dot_general(left_mat, right_mat, (((0,), (0,)), ((), ())), preferred_...  10.5 us
    dot_general x8, matrix products, project_block(): jnp.dot(outer_prod, proj_weight, preferred_element_type=jnp.float32)  6.24 us
    while x32, local copies, waits for them, and re-layouts  4.73 us
  transfers between devices with their start and end apart: 2, of which 2 were waited for; matrix products, arithmetic and copies ran while one was open for 2% of the time, Pallas kernels for 0%

commit v1 on v0

--- a/solution.py
+++ b/solution.py
@@ -70,7 +70,9 @@
     group_len = left_piece.shape[0]
     seq_total = group_len * groups
     left_all, right_seq = (
-        lax.all_gather(left_piece, "seq", axis=0, tiled=True),
+        jnp.concatenate(
+            lax.all_to_all(jnp.stack([left_piece] * lax.axis_size("seq")), "seq", 0, 0), axis=0
+        ),
         lax.all_gather(right_piece, "seq", axis=0, tiled=True),
     )
     right_all = gather_right(right_seq)

time: 235 us -> 218 us (0.928)
  waiting for transfers between devices: 89.8 us -> 67.3 us
  blocking collectives: 88.6 us -> 92.3 us
  starting transfers between devices: 0.04 us -> 3.69 us
    all_to_all x0 -> x1, waiting for transfers between devices: none -> 53 us  [on_device(): lax.all_to_all(jnp.stack([left_piece] * lax.axis_size('seq')), 'seq', 0, 0)]
    all_gather x1 -> x0, waiting for transfers between devices: 43 us -> none  [on_device(): lax.all_gather(left_piece, 'seq', axis=0, tiled=True)]
    all_gather x1, waiting for transfers between devices: 46.1 us -> 14.3 us  [gather_right(): return lax.all_gather(right_part, 'row', axis=1, tiled=True)]
    all_to_all x1, blocking collectives: 28.1 us -> 33.4 us  [on_device(): lax.all_to_all(section_one.reshape(run_len, rowseq_count, own_rows, chann...]
    while x32 -> x12, local copies, waits for them, and re-layouts: 4.73 us -> 0.75 us
    all_to_all x0 -> x1, starting transfers between devices: none -> 3.69 us  [on_device(): lax.all_to_all(jnp.stack([left_piece] * lax.axis_size('seq')), 'seq', 0, 0)]
    while x4, local copies, waits for them, and re-layouts: 3.74 us -> 6.77 us  [project_rows(): lax.map(lambda portion: project_block(portion, right_all, proj_weight), p...]
    dot_general x8, matrix products: 10.5 us -> 7.8 us  [project_block(): lax.dot_general(left_mat, right_mat, (((0,), (0,)), ((), ())), preferred_...]
where the time goes in v1:
time: 218 us
  blocking collectives  92.3 us (42%)
  waiting for transfers between devices  67.3 us (31%)
  local copies, waits for them, and re-layouts  18.2 us (8%)
  matrix products  17.7 us (8%)
  between operations  13.6 us (6%)
  other arithmetic  4.69 us (2%)
  starting transfers between devices  3.69 us (2%)
    all_to_all x1, waiting for transfers between devices, on_device(): lax.all_to_all(jnp.stack([left_piece] * lax.axis_size('seq')), 'seq', 0, 0)  53 us
    all_to_all x2, blocking collectives, move_cols(): return lax.all_to_all(tile, 'col', split_axis=0, concat_axis=2, tiled=True)  43.1 us
    all_to_all x1, blocking collectives, on_device(): lax.all_to_all(section_one.reshape(run_len, rowseq_count, own_rows, chann...  33.4 us
    all_gather x1, blocking collectives, on_device(): lax.all_gather(right_piece, 'seq', axis=0, tiled=True)  15.8 us
    all_gather x1, waiting for transfers between devices, gather_right(): return lax.all_gather(right_part, 'row', axis=1, tiled=True)  14.3 us
    dot_general x8, matrix products, project_block(): jnp.dot(outer_prod, proj_weight, preferred_element_type=jnp.float32)  7.86 us
    dot_general x8, matrix products, project_block(): lax.dot_general(left_mat, right_mat, (((0,), (0,)), ((), ())), preferred_...  7.8 us
    while x4, local copies, waits for them, and re-layouts, project_rows(): lax.map(lambda portion: project_block(portion, right_all, proj_weight), p...  6.77 us
  transfers between devices with their start and end apart: 2, of which 2 were waited for; matrix products, arithmetic and copies ran while one was open for 2% of the time, Pallas kernels for 0%

profile of v1, /device:TPU:1, one launch (start us, length us, event | category | flops | bytes accessed | tf_op | source)
XLA Modules:
  0.0 217.7 jit_solution(6159018315559840100)
XLA Ops:
  6.5 15.8 %all_gather.6 = bf16[512,2,128]{2,1,0:T(2,128)(2,1)S(1)} all-gather(bf16[128,2,128]{2,1,0:T(2,128)(2,1)} %param.19), channel_id=1, replica_groups=mesh['row'=16,'col'=8,'seq'=4] {'seq'}, dimensions={0}, use_global_device_ids=true | all-gather | bytes 327680 | tf_op jit(solution)/shard_map/all_gather | solution.py:76
  22.3 0.7 copy.101
  23.1 0.0 all-gather.2.cloned.1.call-update
  23.1 2.9 %stack.2 = bf16[4,128,32,64]{1,3,2,0:T(8,128)(2,1)} broadcast(bf16[128,32,64]{0,2,1:T(8,128)(2,1)} %param.18), dimensions={1,2,3} | broadcast | bytes 2621440 | tf_op jit(solution)/shard_map/stack | solution.py:74
  26.0 3.7 %all-to-all-start = ((bf16[4,128,32,64]{1,3,2,0:T(8,128)(2,1)}), bf16[4,128,32,64]{1,3,2,0:T(8,128)(2,1)S(1)}, u32[]{:S(2)}, u32[]{:S(2)}) async-start(bf16[4,128,32,64]{1,3,2,0:T(8,128)(2,1)} %stack.2), calls=%async_computation | async-start | bytes 4194304 | tf_op jit(solution)/shard_map/all_to_all | solution.py:74
  29.7 53.0 %all-to-all-done = bf16[4,128,32,64]{1,3,2,0:T(8,128)(2,1)S(1)} async-done(((bf16[4,128,32,64]{1,3,2,0:T(8,128)(2,1)}), bf16[4,128,32,64]{1,3,2,0:T(8,128)(2,1)S(1)}, u32[]{:S(2)}, u32[]{:S(2)}) %all-to-all-start) | async-done | bytes 2097184 | tf_op jit(solution)/shard_map/all_to_all | solution.py:74
  82.7 0.2 fusion.68
  82.9 0.7 dynamic-slice_bitcast_fusion.2
  83.6 14.3 %all-gather.2.cloned.1.call-done = bf16[512,32,128]{2,0,1:T(8,128)(2,1)} async-done(((bf16[512,2,128]{2,0,1:T(8,128)(2,1)}), bf16[512,32,128]{2,0,1:T(8,128)(2,1)}) %all-gather.2.cloned.1.call-update) | async-done | bytes 4194320 | tf_op jit(solution)/shard_map/all_gather | solution.py:46
  97.9 4.1 %fusion.67 = (bf16[128,32,128]{2,0,1:T(8,128)(2,1)}, bf16[128,32,128]{2,0,1:T(8,128)(2,1)}, bf16[128,32,128]{2,0,1:T(8,128)(2,1)}, bf16[128,32,128]{2,0,1:T(8,128)(2,1)S(1)}) fusion(bf16[512,32,128]{2,0,1:T(8,128)(2,1)} %all-gather.2.cloned.1.call-done), kind=kLoop, calls=%fused_computation.71 | loop fusion | bytes 8388608 | tf_op jit(solution)/shard_map/slice | solution.py:84
  102.0 0.7 copy.103
  102.7 0.1 broadcast.44.clone.2
  102.8 0.2 copy-done.5
  103.0 3.1 %while.40 = (s32[]{:T(128)}, f32[2,8,128,128]{3,2,1,0:T(8,128)S(1)}, bf16[2,128,32,8]{1,3,0,2:T(8,128)(2,1)S(1)}, bf16[128,32,128]{2,1,0:T(8,128)(2,1)S(1)}, bf16[1024,128]{1,0:T(8,128)(2,1)S(1)}, /*index=5*/s32[]{:T(128)}) while((s32[]{:T(128)}, f32[2,8,128,128]{3,2,1,0:T(8,128)S(1)}, bf16[2,128,32,8]{1,3,0,2:T(8,128)(2,1)S(1)}, ...), condition=%wide.region_1.2_spmd, body=%wide.region_0.1_spmd.sunk | while | flops 537919488 | bytes 6094925 | solution.py:28
  103.0 0.7 convolution_convert_fusion.8
  103.7 0.8 fusion.96
  104.5 0.8 convolution_convert_fusion.8
  105.3 0.8 fusion.96
  106.1 1.9 copy.105
  108.0 0.1 broadcast.44.clone.3
  108.1 4.9 %while.41 = (s32[]{:T(128)}, f32[2,8,128,128]{3,2,1,0:T(8,128)S(1)}, bf16[2,128,32,8]{1,3,0,2:T(8,128)(2,1)}, bf16[128,32,128]{2,1,0:T(8,128)(2,1)S(1)}, bf16[1024,128]{1,0:T(8,128)(2,1)}, /*index=5*/s32[]{:T(128)}) while((s32[]{:T(128)}, f32[2,8,128,128]{3,2,1,0:T(8,128)S(1)}, bf16[2,128,32,8]{1,3,0,2:T(8,128)(2,1)}, ...), condition=%wide.region_3.4_spmd, body=%wide.region_2.3_spmd.sunk | while | flops 537919488 | bytes 7144037 | solution.py:28
  108.1 1.6 convolution_convert_fusion.9
  109.8 0.8 fusion.101
  110.6 0.0 copy-start.6
  110.6 1.6 convolution_convert_fusion.9
  112.2 0.8 fusion.101
  113.0 2.3 %copy.107 = bf16[128,32,128]{2,1,0:T(8,128)(2,1)S(1)} copy(bf16[128,32,128]{2,0,1:T(8,128)(2,1)} %get-tuple-element.259) | data formatting | bytes 2097152 | tf_op jit(solution)/shard_map/while | solution.py:28
  115.3 1.1 broadcast.44.clone.1
  116.4 5.1 %while.42 = (s32[]{:T(128)}, f32[2,8,128,128]{3,2,1,0:T(8,128)}, bf16[2,128,32,8]{1,3,0,2:T(8,128)(2,1)S(1)}, bf16[128,32,128]{2,1,0:T(8,128)(2,1)S(1)}, bf16[1024,128]{1,0:T(8,128)(2,1)}, /*index=5*/s32[]{:T(128)}) while((s32[]{:T(128)}, f32[2,8,128,128]{3,2,1,0:T(8,128)}, bf16[2,128,32,8]{1,3,0,2:T(8,128)(2,1)S(1)}, ...), condition=%wide.region_5.6_spmd, body=%wide.region_4.5_spmd.sunk | while | flops 537919488 | bytes 7144037 | solution.py:28
  116.4 0.7 convolution_convert_fusion.10
  117.2 0.2 copy-done.7
  117.4 1.6 fusion.106
  119.0 0.8 convolution_convert_fusion.10
  119.7 0.2 copy-done.7
  119.9 1.6 fusion.106
  121.5 1.9 copy.109
  123.4 0.1 broadcast.44.clone
  123.5 3.5 %while.43 = (s32[]{:T(128)}, f32[2,8,128,128]{3,2,1,0:T(8,128)S(1)}, bf16[2,128,32,8]{1,3,0,2:T(8,128)(2,1)S(1)}, bf16[128,32,128]{2,1,0:T(8,128)(2,1)S(1)}, bf16[1024,128]{1,0:T(8,128)(2,1)}, /*index=5*/s32[]{:T(128)}) while((s32[]{:T(128)}, f32[2,8,128,128]{3,2,1,0:T(8,128)S(1)}, bf16[2,128,32,8]{1,3,0,2:T(8,128)(2,1)S(1)}, ...), condition=%wide.region_7.8_spmd, body=%wide.region_6.7_spmd.sunk | while | flops 537919488 | bytes 7143529 | solution.py:28
  123.5 0.0 copy-start.8
  123.5 0.7 convolution_convert_fusion.11
  124.3 0.2 copy-done.8
  124.5 0.8 fusion.111
  125.3 0.0 copy-start.8
  125.3 0.8 convolution_convert_fusion.11
  126.0 0.2 copy-done.8
  126.2 0.8 fusion.111
  127.0 0.0 copy-start.3
  127.0 1.8 add_multiply_fusion
  128.9 0.1 add_convert_fusion
  129.0 22.7 %all_to_all.44 = bf16[8,2,128,128]{3,2,1,0:T(8,128)(2,1)S(1)} all-to-all(bf16[8,2,128,128]{3,2,1,0:T(8,128)(2,1)S(1)} %add_convert_fusion), channel_id=1, replica_groups=mesh['row'=16,'col'=8,'seq'=4] {'col'}, dimensions={0} | all-to-all | bytes 1048576 | tf_op jit(solution)/shard_map/all_to_all | solution.py:50
  151.8 0.0 copy-start.2
  151.8 33.4 %all_to_all.45 = bf16[2,64,16,128]{3,2,0,1:T(8,128)(2,1)S(1)} all-to-all(bf16[2,64,16,128]{3,2,0,1:T(8,128)(2,1)S(1)} %copy.112), channel_id=1, replica_groups=mesh['row'=16,'col'=8,'seq'=4] {'row','seq'}, dimensions={1} | all-to-all | bytes 1048576 | tf_op jit(solution)/shard_map/all_to_all | solution.py:91
  185.2 20.4 %all_to_all.46 = bf16[8,8,1,2,16,128]{5,4,3,1,2,0:T(8,128)(2,1)S(1)} all-to-all(bf16[8,8,1,2,16,128]{5,4,3,1,2,0:T(8,128)(2,1)S(1)} %bitcast.205), channel_id=1, replica_groups=mesh['row'=16,'col'=8,'seq'=4] {'col'}, dimensions={0} | all-to-all | bytes 1048576 | tf_op jit(solution)/shard_map/all_to_all | solution.py:50
  205.6 0.1 bitcast_convert_fusion
  205.8 1.0 fusion.60
  206.8 0.3 convert_reduce_fusion
  207.2 0.1 copy.115
  207.3 0.1 copy.116
  207.3 0.1 copy.117
  207.5 0.6 multiply_reduce_fusion
  208.1 0.1 copy.118
  208.2 0.0 copy-done.4
  208.2 0.6 fusion.63
  208.8 2.0 fusion.57
  (25 shorter events, 0.2 us)
Async XLA Ops:
  6.5 202.3 %copy-start = (bf16[512,128]{1,0:T(8,128)(2,1)S(1)}, bf16[512,128]{1,0:T(8,128)(2,1)}, u32[]{:S(2)}) copy-start(bf16[512,128]{1,0:T(8,128)(2,1)} %param.26) | copy-start | bytes 393220
  6.5 91.4 %all-gather.2.cloned.1.call-start = ((), (), s32[]{:S(2)}) async-start(), calls=%async_computation.4 | async-start | bytes 4456448 | tf_op jit(solution)/shard_map/all_gather | solution.py:46
  26.0 56.7 %all-to-all-start = ((bf16[4,128,32,64]{1,3,2,0:T(8,128)(2,1)}), bf16[4,128,32,64]{1,3,2,0:T(8,128)(2,1)S(1)}, u32[]{:S(2)}, u32[]{:S(2)}) async-start(bf16[4,128,32,64]{1,3,2,0:T(8,128)(2,1)} %stack.2), calls=%async_computation | async-start | bytes 4194304 | tf_op jit(solution)/shard_map/all_to_all | solution.py:74
  102.0 0.9 copy-start.5
  108.1 1.6 copy-start.6
  110.6 1.6 copy-start.6
  113.0 3.4 %copy-start.1 = (f32[2,8,128,128]{3,2,1,0:T(8,128)}, f32[2,8,128,128]{3,2,1,0:T(8,128)S(1)}, u32[]{:S(2)}) copy-start(f32[2,8,128,128]{3,2,1,0:T(8,128)S(1)} %get-tuple-element.114) | copy-start | bytes 3145732
  116.4 1.0 copy-start.7
  119.0 0.9 copy-start.7
  123.5 1.0 copy-start.8
  125.3 1.0 copy-start.8
  127.0 1.9 copy-start.3
  151.8 54.0 %copy-start.2 = (bf16[16,128,128]{2,1,0:T(8,128)(2,1)S(1)}, bf16[16,128,128]{2,1,0:T(8,128)(2,1)}, u32[]{:S(2)}) copy-start(bf16[16,128,128]{2,1,0:T(8,128)(2,1)} %param.22) | copy-start | bytes 1572868
  206.8 1.4 copy-start.4
  207.1 1.7 copy-start.9
  207.1 1.7 copy-start.10
  207.2 1.7 copy-start.11
Sparse Core Ops, SparseCore 0:
  23.2 74.6 all-gather.1
